TPU v7x, 32 devices: a whole 2x2x4 slice. The times are simulated.
32 devices in a mesh: comp: 2 (over core), gx: 4 (over y, x), gy: 4 (over z).
Axes of the slice: x: 2, y: 2, z: 4, core: 2. Of those that a mesh axis runs over, the one named last changes fastest.
Arguments:
- state: float32 [2, 8, 96, 3072], P('comp', None, 'gx', 'gy'), may hold values from -6 to 6
- response: float32 [2, 8, 3072], P('comp'), may hold values from -0.95 to 0
- diffusion: float32 [2, 96, 3072], P('comp', 'gx', 'gy'), may hold values from 0.02 to 0.24
- land_mask: int32 [96, 3072], P('gx', 'gy'), may hold values 0 or 1
- couple_src: int32 [2, 4, 4, 16, 128], P('comp', 'gx', 'gy'), may hold values from 0 to 18431
- couple_dst: int32 [2, 4, 4, 16, 128], P('comp', 'gx', 'gy'), may hold values from 0 to 18431
- couple_weight: float32 [2, 4, 4, 16, 128], P('comp', 'gx', 'gy'), may hold values from 0.1 to 1
- couple_count: int32 [2, 4, 4, 16], P('comp', 'gx', 'gy'), may hold values from 0 to 128, as said below
Outputs:
- final_state: float32 [2, 8, 96, 3072], P('comp', None, 'gx', 'gy')
Inputs may be any that keep to these rules, and one draw needn't show every extreme that they name: `couple_count`: at most 128 live slots per ordered device pair; every sending device has one pair with exactly 128.
All inputs are finite; a program needn't handle non-finite values. No bound on the sum of `land_mask` on one device may be relied on, other than what follows from the above.
Results may differ from a plain program's by a relative error of at most 0.0095.
Values may be sent and summed in bfloat16 or wider, within the bound.
A program may use at most 128 MiB of HBM per device.

v0:
```python
import math
import jax
import jax.numpy as jnp
from jax import lax
from jax.sharding import PartitionSpec as P

FC = 4


def extended(block, sides, width):
    for axis, dim in sides:
        count = lax.axis_size(axis)
        forward = [(i, i + 1) for i in range(count - 1)]
        backward = [(target, source) for source, target in forward]
        low = lax.ppermute(
            lax.slice_in_dim(block, block.shape[dim] - width, None, axis=dim), axis, forward
        )
        high = lax.ppermute(lax.slice_in_dim(block, 0, width, axis=dim), axis, backward)
        block = jnp.concatenate([low, block, high], axis=dim)
    return block


def partner(value, axis, stride):
    mask = 2**stride
    pairs = [(source, source ^ mask) for source in range(lax.axis_size(axis))]
    return lax.ppermute(value, axis, pairs)


def make_table(cols):
    rows_idx = jnp.arange(cols, dtype=jnp.int32)[:, None]
    wave_idx = jnp.arange(cols // 2, dtype=jnp.int32)[None, :]
    phase = rows_idx * wave_idx % cols
    angle = phase.astype(jnp.float32) * (2.0 * math.pi / cols)
    return jnp.concatenate([jnp.cos(angle), jnp.sin(angle)], axis=1).astype(jnp.bfloat16)


def back_transform(filtered, table_part):
    return lax.dot_general(
        filtered, table_part, (((1,), (1,)), ((), ())), preferred_element_type=jnp.float32
    )


def circle_increment(circles, resp_part, table, scale):
    count, rows_part, cols_all = circles.shape
    spec = jnp.dot(circles.reshape(-1, cols_all), table, preferred_element_type=jnp.float32)
    spec = spec.reshape(count, rows_part, cols_all)
    filtered = (spec * resp_part[:, None, :]).astype(jnp.bfloat16)
    incr = (back_transform(filtered.reshape(-1, cols_all), table) * scale).astype(jnp.bfloat16)
    return incr.reshape(count, rows_part, cols_all)


def diffuse(fields, rate):
    padded = extended(fields.astype(jnp.bfloat16), (("gx", 1),), 1).astype(fields.dtype)
    return fields + rate[None] * (padded[:, 2:] + padded[:, :-2] - 2.0 * fields)


def local(
    state, response, diffusion, land_mask, couple_src, couple_dst, couple_weight, couple_count
):
    levels, rows_dev, cols_dev = (state.shape[1], state.shape[2], state.shape[3])
    groups_x = lax.axis_size("gx")
    groups_y = lax.axis_size("gy")
    peers = groups_x * groups_y
    slots = couple_src.shape[4]
    cells = rows_dev * cols_dev
    cols_all = cols_dev * groups_y
    per_level = levels // groups_y
    section = lax.axis_index("comp")
    keep = jnp.where(section == 1, land_mask.astype(jnp.float32), jnp.float32(1.0))
    table = make_table(cols_all)
    scale = 2.0 / cols_all
    src_idx = couple_src.reshape(peers, slots)
    dst_idx = couple_dst.reshape(peers, slots)
    live = jnp.arange(slots, dtype=jnp.int32)[None, :] < couple_count.reshape(peers, 1)
    weights = jnp.where(live, couple_weight.reshape(peers, slots), jnp.float32(0.0))
    first_level = lax.axis_index("gy") * per_level
    resp_mine = lax.dynamic_slice_in_dim(response[0], first_level, per_level, 0)
    rate = diffusion[0]
    fields = state[0]
    surface = fields[:FC].reshape(FC, cells)
    outgoing = jnp.transpose(surface[:, src_idx] * weights[None], (1, 0, 2))
    crossed = partner(outgoing, "comp", 0)
    arrived = lax.all_to_all(crossed, ("gx", "gy"), split_axis=0, concat_axis=0, tiled=True)
    incoming = jnp.transpose(arrived, (1, 0, 2))
    surface = surface.at[:, dst_idx].add(incoming)
    surf = surface.reshape(FC, rows_dev, cols_dev)
    fields = jnp.concatenate([surf, fields[FC:]], axis=0)
    grid_bf = fields.astype(jnp.bfloat16)
    circles = lax.all_to_all(grid_bf, "gy", split_axis=0, concat_axis=2, tiled=True)
    incr = circle_increment(circles, resp_mine, table, scale)
    incr = lax.all_to_all(incr, "gy", split_axis=2, concat_axis=0, tiled=True)
    fields = fields + incr.astype(jnp.float32)
    fields = diffuse(fields, rate) * keep[None]
    return fields[None]


def solution(mesh):
    return jax.shard_map(
        local,
        mesh=mesh,
        in_specs=(
            P("comp", None, "gx", "gy"),
            P("comp", None, None),
            P("comp", "gx", "gy"),
            P("gx", "gy"),
            P("comp", "gx", "gy", None, None),
            P("comp", "gx", "gy", None, None),
            P("comp", "gx", "gy", None, None),
            P("comp", "gx", "gy", None),
        ),
        out_specs=P("comp", None, "gx", "gy"),
        check_vma=False,
    )
```

profile of v0, /device:TPU:4, one launch (start us, length us, event | category | flops | bytes accessed | tf_op | source)
XLA Modules:
  0.0 198.0 jit_solution(5701691548152781341)
XLA Ops:
  0.0 1.1 fusion.28
  1.2 5.6 %copy.20 = f32[1,4,24,768]{1,3,2,0:T(8,128)} copy(f32[1,4,24,768]{3,2,1,0:T(8,128)S(1)} %get-tuple-element.5) | data formatting | bytes 589824 | tf_op jit(solution)/shard_map/slice | solution.py:80
  6.8 9.1 %gather_fusion = f32[2048,4]{1,0:T(8,128)S(1)} fusion(f32[4,18432]{0,1:T(8,128)} %bitcast.55, s32[2048]{0:T(1024)S(1)} %fusion.25), kind=kCustom, calls=%fused_computation | custom fusion | bytes 73728 | tf_op jit(solution)/shard_map/gather | solution.py:81
  16.0 0.3 copy.21
  16.5 1.2 collective-permute-done
  17.7 0.6 copy.22
  18.3 7.3 %all-to-all-start = ((f32[16,4,128]{2,1,0:T(4,128)}), f32[16,4,128]{2,1,0:T(4,128)S(1)}, u32[]{:S(2)}, u32[]{:S(2)}) async-start(f32[16,4,128]{2,1,0:T(4,128)} %copy.22), calls=%async_computation | async-start | bytes 65536 | tf_op jit(solution)/shard_map/all_to_all | solution.py:83
  25.6 6.1 %all-to-all-done = f32[16,4,128]{2,1,0:T(4,128)S(1)} async-done(((f32[16,4,128]{2,1,0:T(4,128)}), f32[16,4,128]{2,1,0:T(4,128)S(1)}, u32[]{:S(2)}, u32[]{:S(2)}) %all-to-all-start) | async-done | bytes 32800 | tf_op jit(solution)/shard_map/all_to_all | solution.py:83
  31.7 0.4 copy.23
  32.0 17.6 %scatter_fusion = f32[4,18432]{0,1:T(8,128)} fusion(f32[4,18432]{0,1:T(8,128)} %bitcast.56, s32[2048]{0:T(1024)S(1)} %fusion.23, f32[2048,4]{1,0:T(8,128)S(1)} %copy.23), kind=kCustom, calls=%fused_computation.1 | custom fusion | flops 8192 | bytes 106496 | tf_op jit(solution)/shard_map/scatter-add | solution.py:85
  49.7 6.4 %copy.24 = f32[4,24,768]{2,1,0:T(8,128)S(1)} copy(f32[4,24,768]{0,2,1:T(8,128)} %bitcast.57) | data formatting | bytes 589824 | tf_op jit(solution)/shard_map/reshape | solution.py:86
  56.1 0.7 fusion.21
  56.8 3.5 %all-to-all-start.1 = ((bf16[8,24,768]{2,1,0:T(8,128)(2,1)}), bf16[8,24,768]{2,1,0:T(8,128)(2,1)S(1)}, u32[]{:S(2)}, u32[]{:S(2)}) async-start(bf16[8,24,768]{2,1,0:T(8,128)(2,1)} %fusion.21), calls=%async_computation.1 | async-start | bytes 589824 | tf_op jit(solution)/shard_map/all_to_all | solution.py:89
  60.3 79.5 %sine_convert_fusion = (bf16[3072,1536]{1,0:T(8,128)(2,1)}, bf16[3072,1536]{1,0:T(8,128)(2,1)}) fusion(), kind=kLoop, calls=%fused_computation.8 | loop fusion | flops 51904512 | bytes 18874368 | tf_op jit(solution)/shard_map/convert.4
  139.8 0.2 copy.29
  140.0 0.2 dot_general.8
  140.2 8.2 %fusion.12 = bf16[2,24,3072]{2,1,0:T(8,128)(2,1)S(1)} fusion(bf16[2,24,3072]{2,1,0:T(8,128)(2,1)S(1)} %dot_general.8, bf16[3072,1536]{1,0:T(8,128)(2,1)} %get-tuple-element.9, bf16[3072,1536]{1,0:T(8,128)(2,1)} %get-tuple-element.10, f32[2,3072]{1,0:T(2,128)S(1)} %dynamic-slice_bitcast_fusion), kind=kOutput, calls=%fused_computation.17 | convolution fusion | flops 944013312 | bytes 19488768 | tf_op jit(solution)/shard_map/dot_general | solution.py:45
  148.4 9.6 %fusion.15 = bf16[48,3072]{1,0:T(8,128)(2,1)S(1)} fusion(bf16[48,3072]{1,0:T(8,128)(2,1)S(1)} %bitcast.67, bf16[3072,1536]{1,0:T(8,128)(2,1)} %get-tuple-element.9, bf16[3072,1536]{1,0:T(8,128)(2,1)} %get-tuple-element.10), kind=kOutput, calls=%fused_computation.18 | convolution fusion | flops 944013312 | bytes 19464192 | tf_op jit(solution)/shard_map/dot_general | solution.py:38
  158.1 1.9 copy.26
  160.0 2.6 %reshape.148 = bf16[4,2,18432]{2,1,0:T(2,128)(2,1)} reshape(bf16[3072,2,24]{2,1,0:T(2,128)(2,1)S(1)} %bitcast.58) | data formatting | bytes 589824
  162.6 5.0 %all-to-all-start.2 = ((bf16[4,2,18432]{2,1,0:T(2,128)(2,1)}), bf16[4,2,18432]{2,1,0:T(2,128)(2,1)S(1)}, u32[]{:S(2)}, u32[]{:S(2)}) async-start(bf16[4,2,18432]{2,1,0:T(2,128)(2,1)} %reshape.148), calls=%async_computation.2 | async-start | bytes 589824 | tf_op jit(solution)/shard_map/all_to_all | solution.py:91
  167.7 8.3 %all-to-all-done.2 = bf16[4,2,18432]{2,1,0:T(2,128)(2,1)S(1)} async-done(((bf16[4,2,18432]{2,1,0:T(2,128)(2,1)}), bf16[4,2,18432]{2,1,0:T(2,128)(2,1)S(1)}, u32[]{:S(2)}, u32[]{:S(2)}) %all-to-all-start.2) | async-done | bytes 294944 | tf_op jit(solution)/shard_map/all_to_all | solution.py:91
  176.0 3.1 %reshape.149 = bf16[3072,2,24]{2,1,0:T(2,128)(2,1)} reshape(bf16[4,2,18432]{2,1,0:T(2,128)(2,1)S(1)} %all-to-all-done.2) | data formatting | bytes 589824
  179.1 2.5 %convert_bitcast_fusion = f32[4,2,24,768]{2,1,3,0:T(2,128)S(1)} fusion(bf16[2,24,4,768]{1,0,3,2:T(2,128)(2,1)} %bitcast.59), kind=kLoop, calls=%fused_computation.19 | loop fusion | flops 147456 | bytes 884736 | tf_op jit(solution)/shard_map/convert_element_type | solution.py:92
  181.6 2.8 %copy.27 = f32[4,2,24,768]{3,2,1,0:T(8,128)} copy(f32[4,2,24,768]{2,1,3,0:T(2,128)S(1)} %convert_bitcast_fusion) | data formatting | bytes 1179648 | tf_op jit(solution)/shard_map/convert_element_type | solution.py:92
  184.4 1.2 fusion.22
  185.7 3.4 %collective-permute-start.2 = (bf16[8,1,768]{2,1,0:T(2,128)(2,1)S(1)}, bf16[8,1,768]{2,1,0:T(2,128)(2,1)S(1)}, u32[]{:S(2)}, u32[]{:S(2)}) collective-permute-start(bf16[8,1,768]{2,1,0:T(2,128)(2,1)S(1)} %get-tuple-element.8), channel_id=1, source_target_pairs={{4,0},{8,4},{12,8},{5,1},{9,5},{13,9},{6,2},{10,6},{14,10},{7,3},{... | collective-permute-start | bytes 36872 | tf_op jit(solution)/shard_map/ppermute | solution.py:18
  189.0 2.5 %collective-permute-start.1 = (bf16[8,1,768]{2,1,0:T(2,128)(2,1)S(1)}, bf16[8,1,768]{2,1,0:T(2,128)(2,1)S(1)}, u32[]{:S(2)}, u32[]{:S(2)}) collective-permute-start(bf16[8,1,768]{2,1,0:T(2,128)(2,1)S(1)} %get-tuple-element.7), channel_id=1, source_target_pairs={{0,4},{4,8},{8,12},{1,5},{5,9},{9,13},{2,6},{6,10},{10,14},{3,7},{... | collective-permute-start | bytes 36872 | tf_op jit(solution)/shard_map/ppermute | solution.py:15
  191.5 0.9 convert_select_fusion
  192.4 3.2 %collective-permute-done.1 = bf16[8,1,768]{2,1,0:T(2,128)(2,1)S(1)} collective-permute-done((bf16[8,1,768]{2,1,0:T(2,128)(2,1)S(1)}, bf16[8,1,768]{2,1,0:T(2,128)(2,1)S(1)}, u32[]{:S(2)}, u32[]{:S(2)}) %collective-permute-start.1) | collective-permute-done | bytes 12320 | tf_op jit(solution)/shard_map/ppermute | solution.py:15
  195.7 0.1 maximum_convert_fusion
  195.8 2.2 %fusion.20 = f32[1,8,24,768]{3,2,1,0:T(8,128)} fusion(f32[8,26,768]{2,1,0:T(8,128)S(1)} %maximum_convert_fusion, f32[24,768]{1,0:T(8,128)S(1)} %convert_select_fusion, f32[24,768]{1,0:T(8,128)} %bitcast.65, f32[4,2,24,768]{3,2,1,0:T(8,128)} %copy.27, f32[4,24,768]{2,1,0:T(8,128)} %copy-done.1, f32[4,24,768]{2,1,0:T(8,128)S(1)} %copy.24), kind=kLoop, calls=%fused_computation.25 | loop fusion | flops 1179648 | bytes 3096576 | tf_op jit(solution)/shard_map/broadcast_in_dim | solution.py:94
  (21 shorter events, 0.2 us)
Async XLA Ops:
  0.0 139.8 %copy-start = (f32[1,8,3072]{2,1,0:T(8,128)S(1)}, f32[1,8,3072]{2,1,0:T(8,128)}, u32[]{:S(2)}) copy-start(f32[1,8,3072]{2,1,0:T(8,128)} %param.9) | copy-start | bytes 294916
  0.0 6.8 %copy-start.2 = (s32[1,1,1,16,128]{4,3,2,1,0:T(8,128)S(1)}, s32[1,1,1,16,128]{4,3,2,1,0:T(8,128)}, u32[]{:S(2)}) copy-start(s32[1,1,1,16,128]{4,3,2,1,0:T(8,128)} %param.12) | copy-start | bytes 24580
  0.0 16.3 %copy-start.3 = (f32[1,1,1,16,128]{4,3,2,1,0:T(8,128)S(1)}, f32[1,1,1,16,128]{4,3,2,1,0:T(8,128)}, u32[]{:S(2)}) copy-start(f32[1,1,1,16,128]{4,3,2,1,0:T(8,128)} %param.14) | copy-start | bytes 24580
  0.0 16.3 %copy-start.5 = (s32[1,1,1,16]{3,2,1,0:T(1,128)S(1)}, s32[1,1,1,16]{3,2,1,0:T(1,128)}, u32[]{:S(2)}) copy-start(s32[1,1,1,16]{3,2,1,0:T(1,128)} %param.15) | copy-start | bytes 196
  0.0 25.6 %copy-start.4 = (s32[1,1,1,16,128]{4,3,2,1,0:T(8,128)S(1)}, s32[1,1,1,16,128]{4,3,2,1,0:T(8,128)}, u32[]{:S(2)}) copy-start(s32[1,1,1,16,128]{4,3,2,1,0:T(8,128)} %param.13) | copy-start | bytes 24580
  1.2 54.9 %copy-start.1 = (f32[4,24,768]{2,1,0:T(8,128)}, f32[4,24,768]{2,1,0:T(8,128)S(1)}, u32[]{:S(2)}) copy-start(f32[4,24,768]{2,1,0:T(8,128)S(1)} %get-tuple-element.6) | copy-start | bytes 884740
  16.4 1.3 collective-permute-start
  18.3 13.4 %all-to-all-start = ((f32[16,4,128]{2,1,0:T(4,128)}), f32[16,4,128]{2,1,0:T(4,128)S(1)}, u32[]{:S(2)}, u32[]{:S(2)}) async-start(f32[16,4,128]{2,1,0:T(4,128)} %copy.22), calls=%async_computation | async-start | bytes 65536 | tf_op jit(solution)/shard_map/all_to_all | solution.py:83
  56.8 83.0 %all-to-all-start.1 = ((bf16[8,24,768]{2,1,0:T(8,128)(2,1)}), bf16[8,24,768]{2,1,0:T(8,128)(2,1)S(1)}, u32[]{:S(2)}, u32[]{:S(2)}) async-start(bf16[8,24,768]{2,1,0:T(8,128)(2,1)} %fusion.21), calls=%async_computation.1 | async-start | bytes 589824 | tf_op jit(solution)/shard_map/all_to_all | solution.py:89
  162.6 13.3 %all-to-all-start.2 = ((bf16[4,2,18432]{2,1,0:T(2,128)(2,1)}), bf16[4,2,18432]{2,1,0:T(2,128)(2,1)S(1)}, u32[]{:S(2)}, u32[]{:S(2)}) async-start(bf16[4,2,18432]{2,1,0:T(2,128)(2,1)} %reshape.148), calls=%async_computation.2 | async-start | bytes 589824 | tf_op jit(solution)/shard_map/all_to_all | solution.py:91
  185.7 6.8 %collective-permute-start.2 = (bf16[8,1,768]{2,1,0:T(2,128)(2,1)S(1)}, bf16[8,1,768]{2,1,0:T(2,128)(2,1)S(1)}, u32[]{:S(2)}, u32[]{:S(2)}) collective-permute-start(bf16[8,1,768]{2,1,0:T(2,128)(2,1)S(1)} %get-tuple-element.8), channel_id=1, source_target_pairs={{4,0},{8,4},{12,8},{5,1},{9,5},{13,9},{6,2},{10,6},{14,10},{7,3},{... | collective-permute-start | bytes 36872 | tf_op jit(solution)/shard_map/ppermute | solution.py:18
  189.0 6.6 %collective-permute-start.1 = (bf16[8,1,768]{2,1,0:T(2,128)(2,1)S(1)}, bf16[8,1,768]{2,1,0:T(2,128)(2,1)S(1)}, u32[]{:S(2)}, u32[]{:S(2)}) collective-permute-start(bf16[8,1,768]{2,1,0:T(2,128)(2,1)S(1)} %get-tuple-element.7), channel_id=1, source_target_pairs={{0,4},{4,8},{8,12},{1,5},{5,9},{9,13},{2,6},{6,10},{10,14},{3,7},{... | collective-permute-start | bytes 36872 | tf_op jit(solution)/shard_map/ppermute | solution.py:15
where the time goes:
time: 199 us; the launch traced here: 198 us
  other arithmetic  105 us (53%)
  local copies, waits for them, and re-layouts  34.5 us (17%)
  starting transfers between devices  21.7 us (11%)
  waiting for transfers between devices  18.8 us (9%)
  matrix products  17.8 us (9%)
    another operation x1, other arithmetic  79.5 us
    scatter-add x1, other arithmetic, local(): surface = surface.at[:, dst_idx].add(incoming)  17.6 us
    dot_general x1, matrix products, back_transform(): lax.dot_general(filtered, table_part, (((1,), (1,)), ((), ())), preferred...  9.63 us
    gather x2, local copies, waits for them, and re-layouts, local(): outgoing = jnp.transpose(surface[:, src_idx] * weights[None], (1, 0, 2))  9.47 us
    all_to_all x1, waiting for transfers between devices, local(): incr = lax.all_to_all(incr, 'gy', split_axis=2, concat_axis=0, tiled=True)  8.3 us
    dot_general x1, matrix products, circle_increment(): jnp.dot(circles.reshape(-1, cols_all), table, preferred_element_type=jnp....  8.22 us
    all_to_all x1, starting transfers between devices, local(): lax.all_to_all(crossed, ('gx', 'gy'), split_axis=0, concat_axis=0, tiled=...  7.28 us
    slice x2, local copies, waits for them, and re-layouts, local(): surface = fields[:FC].reshape(FC, cells)  6.78 us
  transfers between devices with their start and end apart: 6, of which 4 were waited for; matrix products, arithmetic and copies ran while one was open for 41% of the time, Pallas kernels for 0%

commit v1 on v0

--- a/solution.py
+++ b/solution.py
@@ -5,6 +5,29 @@
 from jax.sharding import PartitionSpec as P
 
 FC = 4
+
+
+def in_blocks(x, dim, size):
+    dims = x.shape
+    blocks = x.reshape(*dims[:dim], size, dims[dim] // size, *dims[dim + 1 :])
+    return jnp.moveaxis(blocks, dim, 0)
+
+
+def in_order(blocks, dim):
+    blocks = jnp.moveaxis(blocks, 0, dim)
+    shape = blocks.shape
+    return blocks.reshape(*shape[:dim], shape[dim] * shape[dim + 1], *shape[dim + 2 :])
+
+
+def swapped_with_each(x, axis, split_dim, concat_dim):
+    length, position = (lax.axis_size(axis), lax.axis_index(axis))
+    blocks = in_blocks(x, split_dim, length)
+    gathered = [blocks[position]]
+    for step in range(1, length):
+        sent = blocks[position ^ step]
+        gathered.append(lax.ppermute(sent, axis, [(i, i ^ step) for i in range(length)]))
+    blocks = jnp.stack(gathered)[position ^ jnp.arange(length)]
+    return in_order(blocks, concat_dim)
 
 
 def extended(block, sides, width):
@@ -88,7 +111,7 @@
     grid_bf = fields.astype(jnp.bfloat16)
     circles = lax.all_to_all(grid_bf, "gy", split_axis=0, concat_axis=2, tiled=True)
     incr = circle_increment(circles, resp_mine, table, scale)
-    incr = lax.all_to_all(incr, "gy", split_axis=2, concat_axis=0, tiled=True)
+    incr = swapped_with_each(incr, "gy", 2, 0)
     fields = fields + incr.astype(jnp.float32)
     fields = diffuse(fields, rate) * keep[None]
     return fields[None]

time: 199 us -> 187 us (0.940)
  local copies, waits for them, and re-layouts: 34.5 us -> 25.5 us
  other arithmetic: 105 us -> 99.5 us
  waiting for transfers between devices: 18.8 us -> 22.7 us
    all_to_all x1, waiting for transfers between devices: 0.01 us -> 9.16 us  [local(): lax.all_to_all(grid_bf, 'gy', split_axis=0, concat_axis=2, tiled=True)]
    all_to_all x1 -> x0, waiting for transfers between devices: 8.3 us -> none  [local(): incr = lax.all_to_all(incr, 'gy', split_axis=2, concat_axis=0, tiled=True)]
    unnamed x14 -> x18, local copies, waits for them, and re-layouts: 5.79 us -> 0.08 us
    all_to_all x1 -> x0, starting transfers between devices: 5.04 us -> none  [local(): incr = lax.all_to_all(incr, 'gy', split_axis=2, concat_axis=0, tiled=True)]
    ppermute x0 -> x3, starting transfers between devices: none -> 4.58 us  [swapped_with_each(): lax.ppermute(sent, axis, [(i, i ^ step) for i in range(length)])]
    ppermute x0 -> x3, waiting for transfers between devices: none -> 3.49 us  [swapped_with_each(): lax.ppermute(sent, axis, [(i, i ^ step) for i in range(length)])]
    convert_element_type x1 -> x0, local copies, waits for them, and re-layouts: 2.83 us -> none  [local(): fields = fields + incr.astype(jnp.float32)]
    convert_element_type x1 -> x0, other arithmetic: 2.49 us -> none  [local(): fields = fields + incr.astype(jnp.float32)]
  transfers between devices with their start and end apart: 6 -> 8, of which waited for: 4 -> 5; matrix products, arithmetic and copies ran while one was open for 41% -> 43% of each run, Pallas kernels for 0% -> 0%
where the time goes in v1:
time: 187 us
  other arithmetic  99.5 us (53%)
  local copies, waits for them, and re-layouts  25.5 us (14%)
  waiting for transfers between devices  22.7 us (12%)
  starting transfers between devices  21.2 us (11%)
  matrix products  17.9 us (10%)
    another operation x1, other arithmetic  79.6 us
    scatter-add x1, other arithmetic, local(): surface = surface.at[:, dst_idx].add(incoming)  17.8 us
    dot_general x1, matrix products, back_transform(): lax.dot_general(filtered, table_part, (((1,), (1,)), ((), ())), preferred...  9.66 us
    gather x2, local copies, waits for them, and re-layouts, local(): outgoing = jnp.transpose(surface[:, src_idx] * weights[None], (1, 0, 2))  9.54 us
    all_to_all x1, waiting for transfers between devices, local(): lax.all_to_all(grid_bf, 'gy', split_axis=0, concat_axis=2, tiled=True)  9.16 us
    dot_general x1, matrix products, circle_increment(): jnp.dot(circles.reshape(-1, cols_all), table, preferred_element_type=jnp....  8.21 us
    all_to_all x1, starting transfers between devices, local(): lax.all_to_all(crossed, ('gx', 'gy'), split_axis=0, concat_axis=0, tiled=...  7.28 us
    slice x2, local copies, waits for them, and re-layouts, local(): surface = fields[:FC].reshape(FC, cells)  6.74 us
  transfers between devices with their start and end apart: 8, of which 5 were waited for; matrix products, arithmetic and copies ran while one was open for 43% of the time, Pallas kernels for 0%

profile of v1, /device:TPU:4, one launch (start us, length us, event | category | flops | bytes accessed | tf_op | source)
XLA Modules:
  0.0 187.1 jit_solution(11120111845295750813)
XLA Ops:
  0.0 1.1 fusion.29
  1.1 5.6 %copy.28 = f32[1,4,24,768]{1,3,2,0:T(8,128)} copy(f32[1,4,24,768]{3,2,1,0:T(8,128)S(1)} %get-tuple-element.5) | data formatting | bytes 589824 | tf_op jit(solution)/shard_map/slice | solution.py:103
  6.8 9.2 %gather_fusion = f32[2048,4]{1,0:T(8,128)S(1)} fusion(f32[4,18432]{0,1:T(8,128)} %bitcast.63, s32[2048]{0:T(1024)S(1)} %fusion.25), kind=kCustom, calls=%fused_computation | custom fusion | bytes 73728 | tf_op jit(solution)/shard_map/gather | solution.py:104
  16.0 0.3 copy.29
  16.3 0.1 bitcast_select_fusion
  16.5 79.6 %sine_convert_fusion = (bf16[3072,1536]{1,0:T(8,128)(2,1)}, bf16[3072,1536]{1,0:T(8,128)(2,1)}) fusion(), kind=kLoop, calls=%fused_computation.9 | loop fusion | flops 51904512 | bytes 18874368 | tf_op jit(solution)/shard_map/convert.2
  96.1 0.6 copy.30
  96.7 7.3 %all-to-all-start = ((f32[16,4,128]{2,1,0:T(4,128)}), f32[16,4,128]{2,1,0:T(4,128)S(1)}, u32[]{:S(2)}, u32[]{:S(2)}) async-start(f32[16,4,128]{2,1,0:T(4,128)} %copy.30), calls=%async_computation | async-start | bytes 65536 | tf_op jit(solution)/shard_map/all_to_all | solution.py:106
  104.0 6.0 %all-to-all-done = f32[16,4,128]{2,1,0:T(4,128)S(1)} async-done(((f32[16,4,128]{2,1,0:T(4,128)}), f32[16,4,128]{2,1,0:T(4,128)S(1)}, u32[]{:S(2)}, u32[]{:S(2)}) %all-to-all-start) | async-done | bytes 32800 | tf_op jit(solution)/shard_map/all_to_all | solution.py:106
  110.1 0.4 copy.31
  110.4 17.8 %scatter_fusion = f32[4,18432]{0,1:T(8,128)} fusion(f32[4,18432]{0,1:T(8,128)} %bitcast.64, s32[2048]{0:T(1024)S(1)} %fusion.23, f32[2048,4]{1,0:T(8,128)S(1)} %copy.31), kind=kCustom, calls=%fused_computation.2 | custom fusion | flops 8192 | bytes 106496 | tf_op jit(solution)/shard_map/scatter-add | solution.py:108
  128.2 6.4 %copy.32 = f32[4,24,768]{2,1,0:T(8,128)S(1)} copy(f32[4,24,768]{0,2,1:T(8,128)} %bitcast.65) | data formatting | bytes 589824 | tf_op jit(solution)/shard_map/reshape | solution.py:109
  134.6 0.8 fusion.21
  135.3 3.5 %all-to-all-start.1 = ((bf16[8,24,768]{2,1,0:T(8,128)(2,1)}), bf16[8,24,768]{2,1,0:T(8,128)(2,1)S(1)}, u32[]{:S(2)}, u32[]{:S(2)}) async-start(bf16[8,24,768]{2,1,0:T(8,128)(2,1)} %fusion.21), calls=%async_computation.1 | async-start | bytes 589824 | tf_op jit(solution)/shard_map/all_to_all | solution.py:112
  138.8 9.2 %all-to-all-done.1 = bf16[8,24,768]{2,1,0:T(8,128)(2,1)S(1)} async-done(((bf16[8,24,768]{2,1,0:T(8,128)(2,1)}), bf16[8,24,768]{2,1,0:T(8,128)(2,1)S(1)}, u32[]{:S(2)}, u32[]{:S(2)}) %all-to-all-start.1) | async-done | bytes 294944 | tf_op jit(solution)/shard_map/all_to_all | solution.py:112
  148.0 0.2 copy.47
  148.1 0.2 dot_general.8
  148.3 8.2 %fusion.12 = bf16[2,24,3072]{2,1,0:T(8,128)(2,1)S(1)} fusion(bf16[2,24,3072]{2,1,0:T(8,128)(2,1)S(1)} %dot_general.8, bf16[3072,1536]{1,0:T(8,128)(2,1)} %get-tuple-element.13, bf16[3072,1536]{1,0:T(8,128)(2,1)} %get-tuple-element.14, f32[2,3072]{1,0:T(2,128)S(1)} %dynamic-slice_bitcast_fusion), kind=kOutput, calls=%fused_computation.18 | convolution fusion | flops 944013312 | bytes 19488768 | tf_op jit(solution)/shard_map/dot_general | solution.py:68
  156.6 9.7 %fusion.15 = bf16[48,3072]{1,0:T(8,128)(2,1)S(1)} fusion(bf16[48,3072]{1,0:T(8,128)(2,1)S(1)} %bitcast.79, bf16[3072,1536]{1,0:T(8,128)(2,1)} %get-tuple-element.13, bf16[3072,1536]{1,0:T(8,128)(2,1)} %get-tuple-element.14), kind=kOutput, calls=%fused_computation.19 | convolution fusion | flops 944013312 | bytes 19464192 | tf_op jit(solution)/shard_map/dot_general | solution.py:61
  166.3 0.2 reshape_reshape.3
  166.5 0.6 constant_dynamic-slice_fusion.3
  167.1 1.5 collective-permute-start.3
  168.7 0.1 collective-permute-start.2
  168.8 3.0 %collective-permute-start.1 = (bf16[2,24,768]{2,1,0:T(8,128)(2,1)S(1)}, bf16[2,24,768]{2,1,0:T(8,128)(2,1)S(1)}, u32[]{:S(2)}, u32[]{:S(2)}) collective-permute-start(bf16[2,24,768]{2,1,0:T(8,128)(2,1)S(1)} %bitcast.77), channel_id=1, source_target_pairs={{0,1},{1,0},{2,3},{3,2},{4,5},{5,4},{6,7},{7,6},{8,9},{9,8},{10,11... | collective-permute-start | bytes 221192 | tf_op jit(solution)/shard_map/ppermute | solution.py:28
  171.7 2.2 %collective-permute-done.3 = bf16[2,24,768]{2,1,0:T(8,128)(2,1)S(1)} collective-permute-done((bf16[2,24,768]{2,1,0:T(8,128)(2,1)S(1)}, bf16[2,24,768]{2,1,0:T(8,128)(2,1)S(1)}, u32[]{:S(2)}, u32[]{:S(2)}) %collective-permute-start.3) | collective-permute-done | bytes 73760 | tf_op jit(solution)/shard_map/ppermute | solution.py:28
  174.0 1.3 collective-permute-done.2
  175.3 0.6 gather_fusion.1
  176.0 3.3 %collective-permute-start.5 = (bf16[8,1,768]{2,1,0:T(2,128)(2,1)S(1)}, bf16[8,1,768]{2,1,0:T(2,128)(2,1)S(1)}, u32[]{:S(2)}, u32[]{:S(2)}) collective-permute-start(bf16[8,1,768]{2,1,0:T(2,128)(2,1)S(1)} %get-tuple-element.8), channel_id=1, source_target_pairs={{4,0},{8,4},{12,8},{5,1},{9,5},{13,9},{6,2},{10,6},{14,10},{7,3},{... | collective-permute-start | bytes 36872 | tf_op jit(solution)/shard_map/ppermute | solution.py:41
  179.3 2.6 %collective-permute-start.4 = (bf16[8,1,768]{2,1,0:T(2,128)(2,1)S(1)}, bf16[8,1,768]{2,1,0:T(2,128)(2,1)S(1)}, u32[]{:S(2)}, u32[]{:S(2)}) collective-permute-start(bf16[8,1,768]{2,1,0:T(2,128)(2,1)S(1)} %get-tuple-element.7), channel_id=1, source_target_pairs={{0,4},{4,8},{8,12},{1,5},{5,9},{9,13},{2,6},{6,10},{10,14},{3,7},{... | collective-permute-start | bytes 36872 | tf_op jit(solution)/shard_map/ppermute | solution.py:38
  181.9 4.0 %collective-permute-done.4 = bf16[8,1,768]{2,1,0:T(2,128)(2,1)S(1)} collective-permute-done((bf16[8,1,768]{2,1,0:T(2,128)(2,1)S(1)}, bf16[8,1,768]{2,1,0:T(2,128)(2,1)S(1)}, u32[]{:S(2)}, u32[]{:S(2)}) %collective-permute-start.4) | collective-permute-done | bytes 12320 | tf_op jit(solution)/shard_map/ppermute | solution.py:38
  185.9 0.1 maximum_convert_fusion
  186.0 1.0 fusion.20
  (32 shorter events, 0.4 us)
Async XLA Ops:
  0.0 138.8 %copy-start = (f32[1,8,3072]{2,1,0:T(8,128)S(1)}, f32[1,8,3072]{2,1,0:T(8,128)}, u32[]{:S(2)}) copy-start(f32[1,8,3072]{2,1,0:T(8,128)} %param.9) | copy-start | bytes 294916
  0.0 6.8 %copy-start.3 = (s32[1,1,1,16,128]{4,3,2,1,0:T(8,128)S(1)}, s32[1,1,1,16,128]{4,3,2,1,0:T(8,128)}, u32[]{:S(2)}) copy-start(s32[1,1,1,16,128]{4,3,2,1,0:T(8,128)} %param.12) | copy-start | bytes 24580
  0.0 16.3 %copy-start.4 = (f32[1,1,1,16,128]{4,3,2,1,0:T(8,128)S(1)}, f32[1,1,1,16,128]{4,3,2,1,0:T(8,128)}, u32[]{:S(2)}) copy-start(f32[1,1,1,16,128]{4,3,2,1,0:T(8,128)} %param.14) | copy-start | bytes 24580
  0.0 16.3 %copy-start.6 = (s32[1,1,1,16]{3,2,1,0:T(1,128)S(1)}, s32[1,1,1,16]{3,2,1,0:T(1,128)}, u32[]{:S(2)}) copy-start(s32[1,1,1,16]{3,2,1,0:T(1,128)} %param.15) | copy-start | bytes 196
  16.4 87.6 %copy-start.5 = (s32[1,1,1,16,128]{4,3,2,1,0:T(8,128)S(1)}, s32[1,1,1,16,128]{4,3,2,1,0:T(8,128)}, u32[]{:S(2)}) copy-start(s32[1,1,1,16,128]{4,3,2,1,0:T(8,128)} %param.13) | copy-start | bytes 24580
  16.4 79.6 %collective-permute-start = (f32[16,4,128]{2,0,1:T(8,128)S(1)}, f32[16,4,128]{2,0,1:T(8,128)S(1)}, u32[]{:S(2)}, u32[]{:S(2)}) collective-permute-start(f32[16,4,128]{2,0,1:T(8,128)S(1)} %multiply_bitcast_fusion), channel_id=1, source_target_pairs={{0,16},{16,0},{1,17},{17,1},{2,18},{18,2},{3,19},{19,3},{4,20},{20... | collective-permute-start | bytes 98312 | tf_op jit(solution)/shard_map/ppermute | solution.py:49
  96.7 13.4 %all-to-all-start = ((f32[16,4,128]{2,1,0:T(4,128)}), f32[16,4,128]{2,1,0:T(4,128)S(1)}, u32[]{:S(2)}, u32[]{:S(2)}) async-start(f32[16,4,128]{2,1,0:T(4,128)} %copy.30), calls=%async_computation | async-start | bytes 65536 | tf_op jit(solution)/shard_map/all_to_all | solution.py:106
  135.3 12.7 %all-to-all-start.1 = ((bf16[8,24,768]{2,1,0:T(8,128)(2,1)}), bf16[8,24,768]{2,1,0:T(8,128)(2,1)S(1)}, u32[]{:S(2)}, u32[]{:S(2)}) async-start(bf16[8,24,768]{2,1,0:T(8,128)(2,1)} %fusion.21), calls=%async_computation.1 | async-start | bytes 589824 | tf_op jit(solution)/shard_map/all_to_all | solution.py:112
  156.6 25.3 %copy-start.2 = (s32[24,768]{1,0:T(8,128)S(1)}, s32[24,768]{1,0:T(8,128)}, u32[]{:S(2)}) copy-start(s32[24,768]{1,0:T(8,128)} %param.11) | copy-start | bytes 221188
  156.6 29.4 %copy-start.1 = (f32[1,24,768]{2,1,0:T(8,128)S(1)}, f32[1,24,768]{2,1,0:T(8,128)}, u32[]{:S(2)}) copy-start(f32[1,24,768]{2,1,0:T(8,128)} %param.10) | copy-start | bytes 221188
  167.1 6.8 %collective-permute-start.3 = (bf16[2,24,768]{2,1,0:T(8,128)(2,1)S(1)}, bf16[2,24,768]{2,1,0:T(8,128)(2,1)S(1)}, u32[]{:S(2)}, u32[]{:S(2)}) collective-permute-start(bf16[2,24,768]{2,1,0:T(8,128)(2,1)S(1)} %bitcast.75), channel_id=1, source_target_pairs={{0,3},{1,2},{2,1},{3,0},{4,7},{5,6},{6,5},{7,4},{8,11},{9,10},{10,... | collective-permute-start | bytes 221192 | tf_op jit(solution)/shard_map/ppermute | solution.py:28
  168.7 6.6 %collective-permute-start.2 = (bf16[2,24,768]{2,1,0:T(8,128)(2,1)S(1)}, bf16[2,24,768]{2,1,0:T(8,128)(2,1)S(1)}, u32[]{:S(2)}, u32[]{:S(2)}) collective-permute-start(bf16[2,24,768]{2,1,0:T(8,128)(2,1)S(1)} %bitcast.76), channel_id=1, source_target_pairs={{0,2},{1,3},{2,0},{3,1},{4,6},{5,7},{6,4},{7,5},{8,10},{9,11},{10,... | collective-permute-start | bytes 221192 | tf_op jit(solution)/shard_map/ppermute | solution.py:28
  168.8 6.5 %collective-permute-start.1 = (bf16[2,24,768]{2,1,0:T(8,128)(2,1)S(1)}, bf16[2,24,768]{2,1,0:T(8,128)(2,1)S(1)}, u32[]{:S(2)}, u32[]{:S(2)}) collective-permute-start(bf16[2,24,768]{2,1,0:T(8,128)(2,1)S(1)} %bitcast.77), channel_id=1, source_target_pairs={{0,1},{1,0},{2,3},{3,2},{4,5},{5,4},{6,7},{7,6},{8,9},{9,8},{10,11... | collective-permute-start | bytes 221192 | tf_op jit(solution)/shard_map/ppermute | solution.py:28
  176.0 5.9 %collective-permute-start.5 = (bf16[8,1,768]{2,1,0:T(2,128)(2,1)S(1)}, bf16[8,1,768]{2,1,0:T(2,128)(2,1)S(1)}, u32[]{:S(2)}, u32[]{:S(2)}) collective-permute-start(bf16[8,1,768]{2,1,0:T(2,128)(2,1)S(1)} %get-tuple-element.8), channel_id=1, source_target_pairs={{4,0},{8,4},{12,8},{5,1},{9,5},{13,9},{6,2},{10,6},{14,10},{7,3},{... | collective-permute-start | bytes 36872 | tf_op jit(solution)/shard_map/ppermute | solution.py:41
  179.3 6.6 %collective-permute-start.4 = (bf16[8,1,768]{2,1,0:T(2,128)(2,1)S(1)}, bf16[8,1,768]{2,1,0:T(2,128)(2,1)S(1)}, u32[]{:S(2)}, u32[]{:S(2)}) collective-permute-start(bf16[8,1,768]{2,1,0:T(2,128)(2,1)S(1)} %get-tuple-element.7), channel_id=1, source_target_pairs={{0,4},{4,8},{8,12},{1,5},{5,9},{9,13},{2,6},{6,10},{10,14},{3,7},{... | collective-permute-start | bytes 36872 | tf_op jit(solution)/shard_map/ppermute | solution.py:38
